TPU v7x, 32 devices: a whole 2x2x4 slice. The times are simulated.
32 devices in a mesh: mp: 2 (over y), survey: 16 (over z, x, core).
Axes of the slice: x: 2, y: 2, z: 4, core: 2. Of those that a mesh axis runs over, the one named last changes fastest.
Arguments:
- model: bfloat16 [64, 64, 128], P(('mp', 'survey')), may hold values from -6 to 6
- observed: bfloat16 [32, 64, 128], P(('mp', 'survey')), may hold values from -6 to 6
- weights: bfloat16 [32, 64, 128], P(('mp', 'survey')), may hold values from 0.29882812 to 3
- sensitivity: bfloat16 [2, 2048, 128, 128], P('mp', 'survey'), may hold values from -0.046875 to 0.046875
- block_rows: int32 [2, 2048], P('mp', 'survey'), may hold values from 0 to 15
- block_cols: int32 [2, 2048], P('mp', 'survey'), may hold values from 0 to 3
- block_count: int32 [2, 16], P('mp', 'survey'), may hold values from 32 to 128, as said below
Outputs:
- gradient: float32 [64, 64, 128], P(('mp', 'survey'))
Inputs may be any that keep to these rules, and one draw needn't show every extreme that they name: `block_count`: some device uses all 128 slots.
All inputs are finite; a program needn't handle non-finite values.
Results may differ from a plain program's by a relative error of at most 0.0017.
Values may be sent and summed in bfloat16 or wider, within the bound.
A program may use at most 64 MiB of HBM per device.

v0:
```python
import jax
import jax.numpy as jnp
from jax import lax
from jax.sharding import PartitionSpec as P

SMOOTH = 0.5


def smoothing(model):
    field_f32 = model.astype(jnp.float32)
    earlier = jnp.concatenate([field_f32[:, :1], field_f32[:, :-1]], axis=1)
    later_step = jnp.concatenate([field_f32[:, 1:], field_f32[:, -1:]], axis=1)
    return SMOOTH * (2.0 * field_f32 - earlier - later_step)


def collect(target_ids, in_use, terms, count):
    spare_ids = jnp.where(in_use, target_ids, count)
    summed = jax.ops.segment_sum(terms, spare_ids, num_segments=count + 1)
    return summed[:count]


def on_device(model, observed, weights, sensitivity, block_rows, block_cols, block_count):
    blocks = sensitivity[0]
    row_ids = block_rows[0]
    col_ids = block_cols[0]
    slots = blocks.shape[0]
    in_use = jnp.arange(slots, dtype=jnp.int32) < block_count[0, 0]
    group_rows = observed.shape[0] * lax.axis_size("survey")
    slab = lax.all_gather(model, "mp", axis=0, tiled=True)
    slab_rows = slab.shape[0]
    picked = jnp.take(slab, col_ids, axis=0)
    terms = jnp.einsum("ktc,krc->ktr", picked, blocks, preferred_element_type=jnp.float32)
    partial_value = collect(row_ids, in_use, terms, group_rows)
    summed = lax.psum(partial_value, "survey")
    seen_data, data_weight = (
        lax.all_gather(observed, "survey", axis=0, tiled=True),
        lax.all_gather(weights, "survey", axis=0, tiled=True),
    )
    residual = (data_weight.astype(jnp.float32) * (summed - seen_data.astype(jnp.float32))).astype(
        jnp.bfloat16
    )
    resid_rows = jnp.take(residual, row_ids, axis=0)
    back_terms = jnp.einsum("ktr,krc->ktc", resid_rows, blocks, preferred_element_type=jnp.float32)
    gradient_slab = collect(col_ids, in_use, back_terms, slab_rows)
    owned = lax.psum_scatter(gradient_slab, "mp", scatter_dimension=0, tiled=True)
    return owned + smoothing(model)


def solution(mesh):
    in_specs = (
        P(("mp", "survey"), None, None),
        P(("mp", "survey"), None, None),
        P(("mp", "survey"), None, None),
        P("mp", "survey", None, None),
        P("mp", "survey"),
        P("mp", "survey"),
        P("mp", "survey"),
    )
    out_specs = P(("mp", "survey"), None, None)
    return jax.shard_map(
        on_device, mesh=mesh, in_specs=in_specs, out_specs=out_specs, check_vma=False
    )
```

profile of v0, /device:TPU:0, one launch (start us, length us, event | category | flops | bytes accessed | tf_op | source)
XLA Modules:
  0.0 170.1 jit_solution(15884253694293784097)
XLA Ops:
  6.5 0.0 all-reduce.2.cloned.1.call-start
  7.2 0.7 compare_and_fusion
  7.9 0.7 fusion.15
  8.5 5.8 %all_gather.10 = bf16[4,64,128]{2,1,0:T(8,128)(2,1)S(1)} all-gather(bf16[2,64,128]{2,1,0:T(8,128)(2,1)} %param.7), channel_id=1, replica_groups=mesh['mp'=2,'survey'=16] {'mp'}, dimensions={0}, use_global_device_ids=true | all-gather | bytes 98304 | tf_op jit(solution)/shard_map/all_gather | solution.py:29
  14.3 0.0 copy-start.3
  14.3 0.9 gather_fusion
  15.3 0.0 copy-done.3
  15.3 7.1 %fusion.2 = f32[128,64,128]{2,1,0:T(8,128)} fusion(bf16[1,128,128,128]{3,2,1,0:T(8,128)(2,1)} %param.10, bf16[128,64,128]{2,1,0:T(8,128)(2,1)S(1)} %gather_fusion, pred[128]{0:T(512)(128)(4,1)S(1)} %compare_and_fusion), kind=kOutput, calls=%fused_computation.6 | convolution fusion | flops 269484032 | bytes 10485888 | tf_op jit(solution)/shard_map/ktc,krc->ktr/dot_general | solution.py:32
  22.4 0.0 copy-start.1
  22.4 0.0 copy-start.2
  22.4 13.5 %scatter_fusion = f32[17,64,128]{2,1,0:T(8,128)S(1)} fusion(f32[17,64,128]{2,1,0:T(8,128)S(1)} %broadcast_in_dim.36, s32[128]{0:T(128)S(1)} %get-tuple-element.10, f32[128,64,128]{2,1,0:T(8,128)} %fusion.2), kind=kCustom, calls=%fused_computation.2 | custom fusion | flops 1048576 | bytes 12583424 | tf_op jit(solution)/shard_map/scatter-add | solution.py:18
  36.0 0.8 slice.28
  36.8 0.0 all-reduce.2.cloned.1.call-update
  36.8 0.0 reduce-scatter.2.cloned.1.call-start
  36.9 0.0 copy-done.1
  36.9 23.0 %all_gather.11 = bf16[16,64,128]{2,1,0:T(8,128)(2,1)S(1)} all-gather(bf16[1,64,128]{2,1,0:T(8,128)(2,1)S(1)} %copy-done.1), channel_id=1, replica_groups=mesh['mp'=2,'survey'=16] {'survey'}, dimensions={0}, use_global_device_ids=true | all-gather | bytes 278528 | tf_op jit(solution)/shard_map/all_gather | solution.py:36
  59.9 0.0 copy-done.2
  59.9 18.2 %all_gather.9 = bf16[16,64,128]{2,1,0:T(8,128)(2,1)S(1)} all-gather(bf16[1,64,128]{2,1,0:T(8,128)(2,1)S(1)} %copy-done.2), channel_id=1, replica_groups=mesh['mp'=2,'survey'=16] {'survey'}, dimensions={0}, use_global_device_ids=true | all-gather | bytes 278528 | tf_op jit(solution)/shard_map/all_gather | solution.py:37
  78.1 50.9 %all-reduce.2.cloned.1.call-done = f32[16,64,128]{2,1,0:T(8,128)} async-done(((f32[16,64,128]{2,1,0:T(8,128)}), f32[16,64,128]{2,1,0:T(8,128)}) %all-reduce.2.cloned.1.call-update) | async-done | bytes 524304 | tf_op jit(solution)/shard_map/psum | solution.py:34
  129.1 1.1 multiply_convert_fusion
  130.2 1.0 gather_fusion.1
  131.2 5.4 %fusion = f32[128,64,128]{2,1,0:T(8,128)} fusion(bf16[1,128,128,128]{3,2,1,0:T(8,128)(2,1)} %param.10, bf16[128,64,128]{2,1,0:T(8,128)(2,1)S(1)} %gather_fusion.1, pred[128]{0:T(512)(128)(4,1)S(1)} %compare_and_fusion.1), kind=kOutput, calls=%fused_computation.4 | convolution fusion | flops 269484032 | bytes 10485888 | tf_op jit(solution)/shard_map/ktr,krc->ktc/dot_general | solution.py:43
  136.6 0.0 copy-start
  136.6 13.6 %scatter_fusion.1 = f32[5,64,128]{2,1,0:T(8,128)S(1)} fusion(f32[5,64,128]{2,1,0:T(8,128)S(1)} %broadcast_in_dim.33, s32[128]{0:T(128)S(1)} %get-tuple-element.12, f32[128,64,128]{2,1,0:T(8,128)} %fusion), kind=kCustom, calls=%fused_computation.3 | custom fusion | flops 1048576 | bytes 12583424 | tf_op jit(solution)/shard_map/scatter-add | solution.py:18
  150.2 0.7 slice.29
  150.9 0.0 reduce-scatter.2.cloned.1.call-update
  150.9 0.0 copy-done
  150.9 10.9 %reduce-scatter.2.cloned.1.call-done = f32[2,64,128]{2,1,0:T(8,128)} async-done(((f32[4,64,128]{2,1,0:T(8,128)}), f32[2,64,128]{2,1,0:T(8,128)}) %reduce-scatter.2.cloned.1.call-update) | async-done | bytes 65552 | tf_op jit(solution)/shard_map/reduce_scatter | solution.py:45
  161.8 1.5 fusion.12
  (8 shorter events, 0.1 us)
Async XLA Ops:
  6.5 122.5 %all-reduce.2.cloned.1.call-start = ((), (), s32[]{:S(2)}) async-start(), calls=%async_computation.1 | async-start | bytes 1048576 | tf_op jit(solution)/shard_map/psum | solution.py:34
  14.3 1.0 copy-start.3
  22.4 14.5 %copy-start.1 = (bf16[1,64,128]{2,1,0:T(8,128)(2,1)S(1)}, bf16[1,64,128]{2,1,0:T(8,128)(2,1)}, u32[]{:S(2)}) copy-start(bf16[1,64,128]{2,1,0:T(8,128)(2,1)} %param.8) | copy-start | bytes 49156
  22.4 37.5 %copy-start.2 = (bf16[1,64,128]{2,1,0:T(8,128)(2,1)S(1)}, bf16[1,64,128]{2,1,0:T(8,128)(2,1)}, u32[]{:S(2)}) copy-start(bf16[1,64,128]{2,1,0:T(8,128)(2,1)} %param.9) | copy-start | bytes 49156
  36.8 125.0 %reduce-scatter.2.cloned.1.call-start = ((), (), s32[]{:S(2)}) async-start(), calls=%async_computation.2 | async-start | bytes 196608 | tf_op jit(solution)/shard_map/reduce_scatter | solution.py:45
  136.6 14.3 %copy-start = (bf16[2,64,128]{2,1,0:T(8,128)(2,1)S(1)}, bf16[2,64,128]{2,1,0:T(8,128)(2,1)}, u32[]{:S(2)}) copy-start(bf16[2,64,128]{2,1,0:T(8,128)(2,1)} %param.7) | copy-start | bytes 98308
Sparse Core Ops, SparseCore 0:
  37.0 92.0 all-reduce.1
  151.0 10.7 reduce-scatter.1
where the time goes:
time: 171 us; the launch traced here: 170 us
  waiting for transfers between devices  61.9 us (36%)
  blocking collectives  47 us (27%)
  other arithmetic  31.1 us (18%)
  between operations  14.2 us (8%)
  matrix products  12.5 us (7%)
  local copies, waits for them, and re-layouts  3.49 us (2%)
    psum x1, waiting for transfers between devices, on_device(): summed = lax.psum(partial_value, 'survey')  50.9 us
    scatter-add x2, other arithmetic, collect(): summed = jax.ops.segment_sum(terms, spare_ids, num_segments=count + 1)  27.1 us
    all_gather x1, blocking collectives, on_device(): lax.all_gather(observed, 'survey', axis=0, tiled=True)  23 us
    all_gather x1, blocking collectives, on_device(): lax.all_gather(weights, 'survey', axis=0, tiled=True)  18.2 us
    reduce_scatter x1, waiting for transfers between devices, on_device(): lax.psum_scatter(gradient_slab, 'mp', scatter_dimension=0, tiled=True)  10.9 us
    dot_general x1, matrix products, on_device(): jnp.einsum('ktc,krc->ktr', picked, blocks, preferred_element_type=jnp.flo...  7.05 us
    all_gather x1, blocking collectives, on_device(): slab = lax.all_gather(model, 'mp', axis=0, tiled=True)  5.79 us
    dot_general x1, matrix products, on_device(): jnp.einsum('ktr,krc->ktc', resid_rows, blocks, preferred_element_type=jnp...  5.4 us
  transfers between devices with their start and end apart: 2, of which 2 were waited for; matrix products, arithmetic and copies ran while one was open for 0% of the time, Pallas kernels for 0%

commit v1 on v0

--- a/solution.py
+++ b/solution.py
@@ -31,7 +31,7 @@
     picked = jnp.take(slab, col_ids, axis=0)
     terms = jnp.einsum("ktc,krc->ktr", picked, blocks, preferred_element_type=jnp.float32)
     partial_value = collect(row_ids, in_use, terms, group_rows)
-    summed = lax.psum(partial_value, "survey")
+    summed = jnp.sum(lax.all_gather(partial_value, "survey"), axis=0)
     seen_data, data_weight = (
         lax.all_gather(observed, "survey", axis=0, tiled=True),
         lax.all_gather(weights, "survey", axis=0, tiled=True),

time: 171 us -> 158 us (0.924)
  waiting for transfers between devices: 61.9 us -> 44.2 us
  other arithmetic: 31.1 us -> 34.3 us
    psum x1 -> x0, waiting for transfers between devices: 50.9 us -> none  [on_device(): summed = lax.psum(partial_value, 'survey')]
    all_gather x0 -> x1, waiting for transfers between devices: none -> 35.3 us  [on_device(): summed = jnp.sum(lax.all_gather(partial_value, 'survey'), axis=0)]
    all_gather x1, blocking collectives: 18.2 us -> 23.6 us  [on_device(): lax.all_gather(weights, 'survey', axis=0, tiled=True)]
    reduce_sum x0 -> x1, other arithmetic: none -> 4.24 us  [on_device(): summed = jnp.sum(lax.all_gather(partial_value, 'survey'), axis=0)]
    all_gather x1, blocking collectives: 23 us -> 19.1 us  [on_device(): lax.all_gather(observed, 'survey', axis=0, tiled=True)]
    reduce_scatter x1, waiting for transfers between devices: 10.9 us -> 8.87 us  [on_device(): lax.psum_scatter(gradient_slab, 'mp', scatter_dimension=0, tiled=True)]
where the time goes in v1:
time: 158 us; the launch traced here: 157 us
  blocking collectives  48.4 us (31%)
  waiting for transfers between devices  44.2 us (28%)
  other arithmetic  34.3 us (22%)
  between operations  14.2 us (9%)
  matrix products  12.5 us (8%)
  local copies, waits for them, and re-layouts  3.54 us (2%)
    all_gather x1, waiting for transfers between devices, on_device(): summed = jnp.sum(lax.all_gather(partial_value, 'survey'), axis=0)  35.3 us
    scatter-add x2, other arithmetic, collect(): summed = jax.ops.segment_sum(terms, spare_ids, num_segments=count + 1)  27.1 us
    all_gather x1, blocking collectives, on_device(): lax.all_gather(weights, 'survey', axis=0, tiled=True)  23.6 us
    all_gather x1, blocking collectives, on_device(): lax.all_gather(observed, 'survey', axis=0, tiled=True)  19.1 us
    reduce_scatter x1, waiting for transfers between devices, on_device(): lax.psum_scatter(gradient_slab, 'mp', scatter_dimension=0, tiled=True)  8.87 us
    dot_general x1, matrix products, on_device(): jnp.einsum('ktc,krc->ktr', picked, blocks, preferred_element_type=jnp.flo...  7.05 us
    all_gather x1, blocking collectives, on_device(): slab = lax.all_gather(model, 'mp', axis=0, tiled=True)  5.79 us
    dot_general x1, matrix products, on_device(): jnp.einsum('ktr,krc->ktc', resid_rows, blocks, preferred_element_type=jnp...  5.4 us
  transfers between devices with their start and end apart: 2, of which 2 were waited for; matrix products, arithmetic and copies ran while one was open for 0% of the time, Pallas kernels for 0%

profile of v1, /device:TPU:0, one launch (start us, length us, event | category | flops | bytes accessed | tf_op | source)
XLA Modules:
  0.0 157.2 jit_solution(17542198511322169304)
XLA Ops:
  6.5 0.0 copy-start.3
  6.5 0.0 all-gather.3.cloned.1.call-start
  7.2 0.7 compare_and_fusion
  7.9 0.7 fusion.15
  8.5 5.8 %all_gather.16 = bf16[4,64,128]{2,1,0:T(8,128)(2,1)S(1)} all-gather(bf16[2,64,128]{2,1,0:T(8,128)(2,1)} %param.7), channel_id=1, replica_groups=mesh['mp'=2,'survey'=16] {'mp'}, dimensions={0}, use_global_device_ids=true | all-gather | bytes 98304 | tf_op jit(solution)/shard_map/all_gather | solution.py:29
  14.3 0.9 gather_fusion
  15.3 0.0 copy-done.3
  15.3 7.1 %fusion.2 = f32[128,64,128]{2,1,0:T(8,128)} fusion(bf16[1,128,128,128]{3,2,1,0:T(8,128)(2,1)} %param.10, bf16[128,64,128]{2,1,0:T(8,128)(2,1)S(1)} %gather_fusion, pred[128]{0:T(512)(128)(4,1)S(1)} %compare_and_fusion), kind=kOutput, calls=%fused_computation.6 | convolution fusion | flops 269484032 | bytes 10485888 | tf_op jit(solution)/shard_map/ktc,krc->ktr/dot_general | solution.py:32
  22.4 0.0 copy-start.1
  22.4 0.0 copy-start.2
  22.4 13.5 %scatter_fusion = f32[17,64,128]{2,1,0:T(8,128)S(1)} fusion(f32[17,64,128]{2,1,0:T(8,128)S(1)} %broadcast_in_dim.36, s32[128]{0:T(128)S(1)} %get-tuple-element.10, f32[128,64,128]{2,1,0:T(8,128)} %fusion.2), kind=kCustom, calls=%fused_computation.2 | custom fusion | flops 1048576 | bytes 12583424 | tf_op jit(solution)/shard_map/scatter-add | solution.py:18
  36.0 0.9 slice.28
  36.9 0.0 all-gather.3.cloned.1.call-update
  36.9 0.0 reduce-scatter.2.cloned.1.call-start
  37.0 0.0 copy-done.1
  37.0 23.6 %all_gather.15 = bf16[16,64,128]{2,1,0:T(8,128)(2,1)S(1)} all-gather(bf16[1,64,128]{2,1,0:T(8,128)(2,1)S(1)} %copy-done.1), channel_id=1, replica_groups=mesh['mp'=2,'survey'=16] {'survey'}, dimensions={0}, use_global_device_ids=true | all-gather | bytes 278528 | tf_op jit(solution)/shard_map/all_gather | solution.py:37
  60.5 0.0 copy-done.2
  60.5 19.1 %all_gather.19 = bf16[16,64,128]{2,1,0:T(8,128)(2,1)S(1)} all-gather(bf16[1,64,128]{2,1,0:T(8,128)(2,1)S(1)} %copy-done.2), channel_id=1, replica_groups=mesh['mp'=2,'survey'=16] {'survey'}, dimensions={0}, use_global_device_ids=true | all-gather | bytes 278528 | tf_op jit(solution)/shard_map/all_gather | solution.py:36
  79.6 35.3 %all-gather.3.cloned.1.call-done = f32[256,64,128]{2,1,0:T(8,128)} async-done(((f32[16,64,128]{2,1,0:T(8,128)}), f32[256,64,128]{2,1,0:T(8,128)}) %all-gather.3.cloned.1.call-update) | async-done | bytes 8388624 | tf_op jit(solution)/shard_map/all_gather | solution.py:34
  114.9 4.2 %reduce_sum.9 = f32[16,64,128]{2,1,0:T(8,128)S(1)} reduce(f32[16,16,64,128]{3,2,1,0:T(8,128)} %bitcast.27, f32[]{:T(128)} %constant.12.clone.1), dimensions={0}, to_apply=%region_1.2 | reduce | flops 1966080 | bytes 8912900 | tf_op jit(solution)/shard_map/reduce_sum | solution.py:34
  119.2 0.1 multiply_convert_fusion
  119.3 1.0 gather_fusion.1
  120.2 5.4 %fusion = f32[128,64,128]{2,1,0:T(8,128)} fusion(bf16[1,128,128,128]{3,2,1,0:T(8,128)(2,1)} %param.10, bf16[128,64,128]{2,1,0:T(8,128)(2,1)S(1)} %gather_fusion.1, pred[128]{0:T(512)(128)(4,1)S(1)} %compare_and_fusion.1), kind=kOutput, calls=%fused_computation.4 | convolution fusion | flops 269484032 | bytes 10485888 | tf_op jit(solution)/shard_map/ktr,krc->ktc/dot_general | solution.py:43
  125.7 0.0 copy-start
  125.7 13.6 %scatter_fusion.1 = f32[5,64,128]{2,1,0:T(8,128)S(1)} fusion(f32[5,64,128]{2,1,0:T(8,128)S(1)} %broadcast_in_dim.33, s32[128]{0:T(128)S(1)} %get-tuple-element.12, f32[128,64,128]{2,1,0:T(8,128)} %fusion), kind=kCustom, calls=%fused_computation.3 | custom fusion | flops 1048576 | bytes 12583424 | tf_op jit(solution)/shard_map/scatter-add | solution.py:18
  139.3 0.7 slice.29
  139.9 0.0 reduce-scatter.2.cloned.1.call-update
  139.9 0.0 copy-done
  140.0 8.9 %reduce-scatter.2.cloned.1.call-done = f32[2,64,128]{2,1,0:T(8,128)} async-done(((f32[4,64,128]{2,1,0:T(8,128)}), f32[2,64,128]{2,1,0:T(8,128)}) %reduce-scatter.2.cloned.1.call-update) | async-done | bytes 65552 | tf_op jit(solution)/shard_map/reduce_scatter | solution.py:45
  148.9 1.5 fusion.12
  (8 shorter events, 0.1 us)
Async XLA Ops:
  6.5 8.8 %copy-start.3 = (s32[1,128]{1,0:T(1,128)S(1)}, s32[1,128]{1,0:T(1,128)}, u32[]{:S(2)}) copy-start(s32[1,128]{1,0:T(1,128)} %param.11) | copy-start | bytes 1540
  6.5 108.4 %all-gather.3.cloned.1.call-start = ((), (), s32[]{:S(2)}) async-start(), calls=%async_computation.2 | async-start | bytes 8912896 | tf_op jit(solution)/shard_map/all_gather | solution.py:34
  22.4 14.6 %copy-start.1 = (bf16[1,64,128]{2,1,0:T(8,128)(2,1)S(1)}, bf16[1,64,128]{2,1,0:T(8,128)(2,1)}, u32[]{:S(2)}) copy-start(bf16[1,64,128]{2,1,0:T(8,128)(2,1)} %param.9) | copy-start | bytes 49156
  22.4 38.1 %copy-start.2 = (bf16[1,64,128]{2,1,0:T(8,128)(2,1)S(1)}, bf16[1,64,128]{2,1,0:T(8,128)(2,1)}, u32[]{:S(2)}) copy-start(bf16[1,64,128]{2,1,0:T(8,128)(2,1)} %param.8) | copy-start | bytes 49156
  36.9 112.0 %reduce-scatter.2.cloned.1.call-start = ((), (), s32[]{:S(2)}) async-start(), calls=%async_computation.1 | async-start | bytes 196608 | tf_op jit(solution)/shard_map/reduce_scatter | solution.py:45
  125.7 14.3 %copy-start = (bf16[2,64,128]{2,1,0:T(8,128)(2,1)S(1)}, bf16[2,64,128]{2,1,0:T(8,128)(2,1)}, u32[]{:S(2)}) copy-start(bf16[2,64,128]{2,1,0:T(8,128)(2,1)} %param.7) | copy-start | bytes 98308
Sparse Core Ops, SparseCore 0:
  37.0 77.8 all-gather.2
  140.1 8.7 reduce-scatter.1
